TPU v7x, 128 devices: a whole 4x4x4 slice. The times are simulated.
128 devices in a mesh: freq: 4 (over z_hi, core), vis: 32 (over z_lo, y, x).
Axes of the slice: x: 4, y: 4, z: 4 (z_hi: 2, z_lo: 2; z = z_hi * 2 + z_lo), core: 2. Of those that a mesh axis runs over, the one named last changes fastest.
Arguments:
- model_input: bfloat16 [2, 16, 512, 512], P(None, 'freq', 'vis'), parts along dimension 1, may hold values from -6 to 6
- w_kernels: bfloat16 [64, 2, 128, 128], P('freq'), parts along dimension 0, may hold values from -0.375 to 0.375
- visibilities: bfloat16 [4096, 2, 128, 128], P(('freq', 'vis')), parts along dimension 0, may hold values from -6 to 6
- tile_facet: int32 [4096], P(('freq', 'vis')), parts along dimension 0, may hold values from 0 to 3
- tile_patch: int32 [4096], P(('freq', 'vis')), parts along dimension 0, may hold values from 0 to 15
- tile_wplane: int32 [4096], P(('freq', 'vis')), parts along dimension 0, may hold values from 0 to 15
- tile_count: int32 [128], P(('freq', 'vis')), parts along dimension 0, may hold values from 16 to 32, as said below
Outputs:
- residual_image: float32 [16, 512, 512], P('freq', 'vis'), parts along dimension 0
There are 4 independent parts, one for each index of `freq`. A program takes and returns all parts, laid end to end along the dimension named above; each array names one. Nothing has to cross between parts.
Inputs may be any that keep to these rules, and one draw needn't show every extreme that they name: `tile_count`: each device's live tiles fill its first slots; some device holds exactly 32.
All inputs are finite; a program needn't handle non-finite values.
Results may differ from a plain program's by a relative error of at most 0.02.
Values may be sent and summed in bfloat16 or wider, within the bound.
A program may use at most 128 MiB of HBM per device.

v0:
```python
import math
import jax
import jax.numpy as jnp
from jax import lax
from jax.sharding import PartitionSpec as P

P_SIZE = 512
S = 128
F = 4
WPLANES = 16
CYCLES = 2
TILE_CAP = 32
NP = 16
loop_gain = 0.5


def dft_tables(first_row, row_count, length):
    row_ids = first_row + jnp.arange(row_count, dtype=jnp.int32)
    col_ids = jnp.arange(length, dtype=jnp.int32)
    phases = row_ids[:, None] * col_ids[None, :] % length
    angles = phases.astype(jnp.float32) * (2.0 * math.pi / length)
    scaling = 1.0 / math.sqrt(length)
    return (jnp.cos(angles) * scaling, jnp.sin(angles) * scaling)


def lowprec(pattern, first_op, second_op):
    return jnp.einsum(pattern, first_op, second_op, preferred_element_type=jnp.float32)


def exact(pattern, first_op, second_op):
    return jnp.einsum(
        pattern,
        first_op,
        second_op,
        precision=lax.Precision.HIGHEST,
        preferred_element_type=jnp.float32,
    )


def column_pass(half_grid, cosine_half, sine_half):
    half_real, half_imag = (half_grid[:, 0], half_grid[:, 1])
    grid_real = lowprec("ij,fjk->fik", cosine_half, half_real) + lowprec(
        "ij,fjk->fik", sine_half, half_imag
    )
    grid_imag = lowprec("ij,fjk->fik", cosine_half, half_imag) - lowprec(
        "ij,fjk->fik", sine_half, half_real
    )
    return jnp.stack([grid_real, grid_imag], axis=1).astype(jnp.bfloat16)


def tile_terms(patches, kernel, observed, alive):
    patch_real, patch_imag = (patches[:, 0], patches[:, 1])
    kern_real, kern_imag = (kernel[:, 0], kernel[:, 1])
    mid_real = (
        lowprec("tij,tjk->tik", kern_real, patch_real)
        - lowprec("tij,tjk->tik", kern_imag, patch_imag)
    ).astype(jnp.bfloat16)
    mid_imag = (
        lowprec("tij,tjk->tik", kern_real, patch_imag)
        + lowprec("tij,tjk->tik", kern_imag, patch_real)
    ).astype(jnp.bfloat16)
    model_real = lowprec("tij,tkj->tik", mid_real, kern_real) - lowprec(
        "tij,tkj->tik", mid_imag, kern_imag
    )
    model_imag = lowprec("tij,tkj->tik", mid_real, kern_imag) + lowprec(
        "tij,tkj->tik", mid_imag, kern_real
    )
    resid_real = ((observed[:, 0].astype(jnp.float32) - model_real) * alive[:, None, None]).astype(
        jnp.bfloat16
    )
    resid_imag = ((observed[:, 1].astype(jnp.float32) - model_imag) * alive[:, None, None]).astype(
        jnp.bfloat16
    )
    back_real = (
        lowprec("tji,tjk->tik", kern_real, resid_real)
        + lowprec("tji,tjk->tik", kern_imag, resid_imag)
    ).astype(jnp.bfloat16)
    back_imag = (
        lowprec("tji,tjk->tik", kern_real, resid_imag)
        - lowprec("tji,tjk->tik", kern_imag, resid_real)
    ).astype(jnp.bfloat16)
    out_real = lowprec("tij,tjk->tik", back_real, kern_real) + lowprec(
        "tij,tjk->tik", back_imag, kern_imag
    )
    out_imag = lowprec("tij,tjk->tik", back_imag, kern_real) - lowprec(
        "tij,tjk->tik", back_real, kern_imag
    )
    return jnp.stack([out_real, out_imag], axis=1).reshape(patches.shape[0], 2 * S * S)


def local(model_input, w_kernels, visibilities, tile_facet, tile_patch, tile_wplane, tile_count):
    devices = lax.axis_size("vis")
    position = lax.axis_index("vis")
    local_rows = P_SIZE // devices
    cosine_full, sine_full = dft_tables(0, P_SIZE, P_SIZE)
    cosine_half = cosine_full.astype(jnp.bfloat16)
    sine_half = sine_full.astype(jnp.bfloat16)
    weight = math.sqrt(F * NP / (TILE_CAP * devices))
    slots = tile_facet * NP + tile_patch
    alive = (jnp.arange(TILE_CAP, dtype=jnp.int32) < tile_count[0]).astype(jnp.float32)
    kernel_table = w_kernels.reshape(WPLANES, 2 * S * S)
    block_count = TILE_CAP // 16
    blocks = (
        slots.reshape(block_count, 16),
        tile_wplane.reshape(block_count, 16),
        visibilities.reshape(block_count, 16, 2, S, S),
        alive.reshape(block_count, 16),
    )
    residual_image = jnp.zeros((F, local_rows, P_SIZE), jnp.float32)
    for cycle_index in range(CYCLES):
        if cycle_index == 0:
            sky_model = model_input[0]
        else:
            sky_model = (
                model_input[cycle_index].astype(jnp.float32) + loop_gain * residual_image
            ).astype(jnp.bfloat16)
        half_real = lowprec("fij,jk->fik", sky_model, cosine_half)
        half_imag = -lowprec("fij,jk->fik", sky_model, sine_half)
        half_grid = jnp.stack([half_real, half_imag], axis=1).astype(jnp.bfloat16)
        column_half = lax.all_to_all(half_grid, "vis", split_axis=3, concat_axis=2, tiled=True)
        grid_part = column_pass(column_half, cosine_half, sine_half)
        full_grid = lax.all_gather(grid_part, "vis", axis=3, tiled=True)
        patch_table = (
            full_grid.reshape(F, 2, P_SIZE // S, S, P_SIZE // S, S)
            .transpose(0, 2, 4, 1, 3, 5)
            .reshape(F * NP, 2 * S * S)
        )

        def accumulate(running, tile_block):
            slot_ids, plane_ids, observed, live_block = tile_block
            choose = (slot_ids[:, None] == jnp.arange(F * NP, dtype=jnp.int32)[None, :]).astype(
                jnp.bfloat16
            )
            patches = (
                jnp.dot(choose, patch_table, preferred_element_type=jnp.float32)
                .astype(jnp.bfloat16)
                .reshape(16, 2, S, S)
            )
            plane_pick = (
                plane_ids[:, None] == jnp.arange(WPLANES, dtype=jnp.int32)[None, :]
            ).astype(jnp.bfloat16)
            kernel = (
                jnp.dot(plane_pick, kernel_table, preferred_element_type=jnp.float32)
                .astype(jnp.bfloat16)
                .reshape(16, 2, S, S)
            )
            tile_sums = tile_terms(patches, kernel, observed, live_block)
            return (running.at[slot_ids].add(tile_sums), None)

        summed, unused = lax.scan(accumulate, jnp.zeros((F * NP, 2 * S * S), jnp.float32), blocks)
        resid_grid = (
            summed.reshape(F, P_SIZE // S, P_SIZE // S, 2, S, S)
            .transpose(0, 3, 1, 4, 2, 5)
            .reshape(F, 2, P_SIZE, P_SIZE)
        )
        total_grid = lax.psum(resid_grid.astype(jnp.bfloat16), "vis").astype(jnp.float32)
        cosine_rows, sine_rows = dft_tables(position * local_rows, local_rows, P_SIZE)
        spec_real = exact("ij,fjk->fik", cosine_rows, total_grid[:, 0]) - exact(
            "ij,fjk->fik", sine_rows, total_grid[:, 1]
        )
        spec_imag = exact("ij,fjk->fik", cosine_rows, total_grid[:, 1]) + exact(
            "ij,fjk->fik", sine_rows, total_grid[:, 0]
        )
        residual_image = (
            exact("fij,jk->fik", spec_real, cosine_full)
            - exact("fij,jk->fik", spec_imag, sine_full)
        ) * weight
    return residual_image


def solution(mesh):
    return jax.shard_map(
        local,
        mesh=mesh,
        in_specs=(
            P(None, "freq", "vis", None),
            P("freq", None, None, None),
            P(("freq", "vis"), None, None, None),
            P(("freq", "vis")),
            P(("freq", "vis")),
            P(("freq", "vis")),
            P(("freq", "vis")),
        ),
        out_specs=P("freq", "vis", None),
        check_vma=False,
    )
```

profile of v0, /device:TPU:0, one launch (start us, length us, event | category | flops | bytes accessed | tf_op | source)
XLA Modules:
  0.0 1282.2 jit_solution(3081509541282992001)
XLA Ops:
  6.5 5.0 fusion.92
  17.6 17.2 %all_to_all.36 = bf16[32,2,1024]{2,1,0:T(2,128)(2,1)S(1)} all-to-all(bf16[32,2,1024]{2,1,0:T(2,128)(2,1)S(1)} %reshape.173), channel_id=1, replica_groups=mesh['freq'=4,'vis'=32] {'vis'}, dimensions={0} | all-to-all | bytes 262144 | tf_op jit(solution)/shard_map/all_to_all | solution.py:120
  46.0 4.4 fusion.90
  59.6 152.0 %all-gather.3.cloned.1.call-done = bf16[4,2,512,512]{2,3,0,1:T(8,128)(2,1)} async-done(((bf16[4,2,512,16]{2,3,0,1:T(8,128)(2,1)}), bf16[4,2,512,512]{2,3,0,1:T(8,128)(2,1)}) %all-gather.3.cloned.1.call-update) | async-done | bytes 4194320 | tf_op jit(solution)/shard_map/all_gather | solution.py:122
  211.6 7.0 reshape.138
  218.5 7.5 copy.83
  226.0 7.3 reshape.139
  237.2 43.1 %while.20 = (s32[]{:T(128)}, f32[64,32768]{1,0:T(8,128)}, s32[2,16]{1,0:T(2,128)S(1)}, s32[2,16]{1,0:T(2,128)S(1)}, bf16[16,32768]{1,0:T(8,128)(2,1)S(1)}, /*ind...) while((s32[]{:T(128)}, f32[64,32768]{1,0:T(8,128)}, ...), condition=%wide.region_2.3_spmd, body=%wide.region_0.2_spmd.sunk | while | flops 1164969216 | bytes 89130760 | solution.py:150
  248.0 10.6 scatter_custom_fusion.9
  269.4 10.6 scatter_custom_fusion.9
  285.6 5.9 copy.143
  291.5 7.2 convert_element_type.191
  298.7 4.4 copy.86
  303.2 321.4 %all-reduce.3.cloned.1.call-done = bf16[4,2,512,512]{3,2,0,1:T(8,128)(2,1)} async-done(((bf16[4,2,512,512]{3,2,0,1:T(8,128)(2,1)}), bf16[4,2,512,512]{3,2,0,1:T(8,128)(2,1)}) %all-reduce.3.cloned.1.call-update) | async-done | bytes 4194320 | tf_op jit(solution)/shard_map/psum | solution.py:156
  630.0 4.9 fusion.103
  637.1 4.7 fusion.81
  641.8 4.5 fusion.93
  646.3 4.5 fusion.94
  652.7 15.9 %all_to_all.37 = bf16[32,2,1024]{2,1,0:T(2,128)(2,1)S(1)} all-to-all(bf16[32,2,1024]{2,1,0:T(2,128)(2,1)S(1)} %reshape.175), channel_id=1, replica_groups=mesh['freq'=4,'vis'=32] {'vis'}, dimensions={0} | all-to-all | bytes 262144 | tf_op jit(solution)/shard_map/all_to_all | solution.py:120
  689.0 155.5 %all-gather.5.cloned.1.call-done = bf16[4,2,512,512]{2,3,0,1:T(8,128)(2,1)} async-done(((bf16[4,2,512,16]{2,3,0,1:T(8,128)(2,1)}), bf16[4,2,512,512]{2,3,0,1:T(8,128)(2,1)}) %all-gather.5.cloned.1.call-update) | async-done | bytes 4194320 | tf_op jit(solution)/shard_map/all_gather | solution.py:122
  844.4 7.1 reshape.140
  851.5 7.5 copy.92
  859.0 7.3 reshape.141
  870.2 42.9 %while.21 = (s32[]{:T(128)}, f32[64,32768]{1,0:T(8,128)}, s32[2,16]{1,0:T(2,128)S(1)}, s32[2,16]{1,0:T(2,128)S(1)}, bf16[16,32768]{1,0:T(8,128)(2,1)S(1)}, /*ind...) while((s32[]{:T(128)}, f32[64,32768]{1,0:T(8,128)}, ...), condition=%wide.region_6.7_spmd, body=%wide.region_4.6_spmd.sunk | while | flops 1164969216 | bytes 89130760 | solution.py:150
  881.0 10.6 scatter_custom_fusion.11
  902.3 10.6 scatter_custom_fusion.11
  918.3 5.9 copy.142
  924.2 7.2 convert_element_type.197
  931.4 4.4 copy.95
  935.9 321.6 %all-reduce.5.cloned.1.call-done = bf16[4,2,512,512]{3,2,0,1:T(8,128)(2,1)} async-done(((bf16[4,2,512,512]{3,2,0,1:T(8,128)(2,1)}), bf16[4,2,512,512]{3,2,0,1:T(8,128)(2,1)}) %all-reduce.5.cloned.1.call-update) | async-done | bytes 4194320 | tf_op jit(solution)/shard_map/psum | solution.py:156
  1262.9 4.7 fusion.101
  1269.8 5.6 fusion.72
  (177 shorter events, 123.6 us)
Async XLA Ops:
  6.5 5.1 copy-start.5
  6.5 205.0 %all-gather.3.cloned.1.call-start = ((), (), s32[]{:S(2)}) async-start(), calls=%async_computation.2 | async-start | bytes 4325376 | tf_op jit(solution)/shard_map/all_gather | solution.py:122
  46.0 9.4 copy-start.4
  54.6 4.8 copy-start.6
  54.6 4.8 copy-start.7
  54.6 4.9 copy-start.8
  55.3 569.2 %all-reduce.3.cloned.1.call-start = ((), (), s32[]{:S(2)}) async-start(), calls=%async_computation.3 | async-start | bytes 8388608 | tf_op jit(solution)/shard_map/psum | solution.py:156
  237.2 2.2 copy-start.1
  258.6 2.2 copy-start.1
  303.1 541.3 %all-gather.5.cloned.1.call-start = ((), (), s32[]{:S(2)}) async-start(), calls=%async_computation.4 | async-start | bytes 4325376 | tf_op jit(solution)/shard_map/all_gather | solution.py:122
  624.6 10.4 copy-start.2
  688.9 568.6 %all-reduce.5.cloned.1.call-start = ((), (), s32[]{:S(2)}) async-start(), calls=%async_computation.5 | async-start | bytes 8388608 | tf_op jit(solution)/shard_map/psum | solution.py:156
  870.2 2.2 copy-start
  891.6 2.2 copy-start
  1257.5 10.2 copy-start.3
Sparse Core Ops, SparseCore 0:
  55.4 156.0 all-gather.2
  303.2 321.2 all-reduce.2
  689.0 155.3 all-gather.4
  936.0 321.3 all-reduce.4
where the time goes:
time: 1290 us; the launch traced here: 1280 us
  waiting for transfers between devices  950 us (74%)
  local copies, waits for them, and re-layouts  116 us (9%)
  matrix products  114 us (9%)
  other arithmetic  52.7 us (4%)
  blocking collectives  33.1 us (3%)
  between operations  14.4 us (1%)
    psum x2, waiting for transfers between devices, local(): lax.psum(resid_grid.astype(jnp.bfloat16), 'vis').astype(jnp.float32)  643 us
    all_gather x2, waiting for transfers between devices, local(): full_grid = lax.all_gather(grid_part, 'vis', axis=3, tiled=True)  307 us
    dot_general x76, matrix products, lowprec(): jnp.einsum(pattern, first_op, second_op, preferred_element_type=jnp.float32)  74.3 us
    scatter-add x4, other arithmetic, accumulate(): return (running.at[slot_ids].add(tile_sums), None)  42.3 us
    dot_general x12, matrix products, exact(): jnp.einsum(pattern, first_op, second_op, precision=lax.Precision.HIGHEST,...  35.2 us
    convert_element_type x6, local copies, waits for them, and re-layouts, local(): resid_grid.astype(jnp.bfloat16)  35.1 us
    all_to_all x2, blocking collectives, local(): lax.all_to_all(half_grid, 'vis', split_axis=3, concat_axis=2, tiled=True)  33.1 us
  transfers between devices with their start and end apart: 4, of which 4 were waited for; matrix products, arithmetic and copies ran while one was open for 0% of the time, Pallas kernels for 0%

commit v1 on v0

--- a/solution.py
+++ b/solution.py
@@ -119,7 +119,10 @@
         half_grid = jnp.stack([half_real, half_imag], axis=1).astype(jnp.bfloat16)
         column_half = lax.all_to_all(half_grid, "vis", split_axis=3, concat_axis=2, tiled=True)
         grid_part = column_pass(column_half, cosine_half, sine_half)
-        full_grid = lax.all_gather(grid_part, "vis", axis=3, tiled=True)
+        size = lax.axis_size("vis")
+        parts = jnp.stack([grid_part for _ in range(size)])
+        parts = lax.all_to_all(parts, "vis", split_axis=0, concat_axis=0)
+        full_grid = jnp.concatenate(parts, axis=3)
         patch_table = (
             full_grid.reshape(F, 2, P_SIZE // S, S, P_SIZE // S, S)
             .transpose(0, 2, 4, 1, 3, 5)

time: 1290 us -> 1080 us (0.84)
  waiting for transfers between devices: 950 us -> 693 us
  blocking collectives: 33.1 us -> 66.6 us
    all_gather x2 -> x0, waiting for transfers between devices: 307 us -> none  [local(): full_grid = lax.all_gather(grid_part, 'vis', axis=3, tiled=True)]
    all_to_all x0 -> x1, waiting for transfers between devices: none -> 47.2 us  [local(): parts = lax.all_to_all(parts, 'vis', split_axis=0, concat_axis=0)]
    all_to_all x0 -> x1, blocking collectives: none -> 33.4 us  [local(): parts = lax.all_to_all(parts, 'vis', split_axis=0, concat_axis=0)]
    another operation x2 -> x8, local copies, waits for them, and re-layouts: 7.8 us -> 25.1 us  [the longest x2 14.2 us: local(): full_grid.reshape(F, 2, P_SIZE // S, S, P_SIZE // S, S)]
  transfers between devices with their start and end apart: 4 -> 3, of which waited for: 4 -> 3; matrix products, arithmetic and copies ran while one was open for 0% -> 0% of each run, Pallas kernels for 0% -> 0%
where the time goes in v1:
time: 1080 us; the launch traced here: 1070 us
  waiting for transfers between devices  693 us (64%)
  local copies, waits for them, and re-layouts  125 us (12%)
  matrix products  114 us (11%)
  blocking collectives  66.6 us (6%)
  other arithmetic  51.4 us (5%)
  between operations  14.7 us (1%)
    psum x2, waiting for transfers between devices, local(): lax.psum(resid_grid.astype(jnp.bfloat16), 'vis').astype(jnp.float32)  646 us
    dot_general x76, matrix products, lowprec(): jnp.einsum(pattern, first_op, second_op, preferred_element_type=jnp.float32)  74.2 us
    all_to_all x1, waiting for transfers between devices, local(): parts = lax.all_to_all(parts, 'vis', split_axis=0, concat_axis=0)  47.2 us
    scatter-add x4, other arithmetic, accumulate(): return (running.at[slot_ids].add(tile_sums), None)  42.3 us
    dot_general x12, matrix products, exact(): jnp.einsum(pattern, first_op, second_op, precision=lax.Precision.HIGHEST,...  35.2 us
    convert_element_type x6, local copies, waits for them, and re-layouts, local(): resid_grid.astype(jnp.bfloat16)  35.1 us
    all_to_all x1, blocking collectives, local(): parts = lax.all_to_all(parts, 'vis', split_axis=0, concat_axis=0)  33.4 us
    all_to_all x2, blocking collectives, local(): lax.all_to_all(half_grid, 'vis', split_axis=3, concat_axis=2, tiled=True)  33.2 us
  transfers between devices with their start and end apart: 3, of which 3 were waited for; matrix products, arithmetic and copies ran while one was open for 0% of the time, Pallas kernels for 0%

profile of v1, /device:TPU:0, one launch (start us, length us, event | category | flops | bytes accessed | tf_op | source)
XLA Modules:
  0.0 1071.2 jit_solution(15086647585049936632)
XLA Ops:
  6.5 5.0 fusion.92
  17.6 17.2 %all_to_all.46 = bf16[32,2,1024]{2,1,0:T(2,128)(2,1)S(1)} all-to-all(bf16[32,2,1024]{2,1,0:T(2,128)(2,1)S(1)} %reshape.195), channel_id=1, replica_groups=mesh['freq'=4,'vis'=32] {'vis'}, dimensions={0} | all-to-all | bytes 262144 | tf_op jit(solution)/shard_map/all_to_all | solution.py:120
  57.1 5.0 all-to-all-start.1
  65.3 47.2 %all-to-all-done.1 = bf16[32,4,2,512,16]{3,4,2,1,0:T(8,128)(2,1)} async-done(((bf16[32,4,2,512,16]{3,4,2,1,0:T(8,128)(2,1)}), bf16[32,4,2,512,16]{3,4,2,1,0:T(8,128)(2,1)}, u32[]{:S(2)}, u32[]{:S(2)}) %all-to-all-start.1) | async-done | bytes 4194336 | tf_op jit(solution)/shard_map/all_to_all | solution.py:124
  112.5 4.8 copy.120
  117.3 7.3 reshape_reshape.6
  124.6 7.5 copy.121
  132.1 7.3 reshape.161
  143.3 42.9 %while.20 = (s32[]{:T(128)}, f32[64,32768]{1,0:T(8,128)}, s32[2,16]{1,0:T(2,128)S(1)}, s32[2,16]{1,0:T(2,128)S(1)}, bf16[16,32768]{1,0:T(8,128)(2,1)S(1)}, /*ind...) while((s32[]{:T(128)}, f32[64,32768]{1,0:T(8,128)}, ...), condition=%wide.region_2.3_spmd, body=%wide.region_0.2_spmd.sunk | while | flops 1164969216 | bytes 89130760 | solution.py:153
  154.1 10.6 scatter_custom_fusion.9
  175.5 10.6 scatter_custom_fusion.9
  191.4 5.9 copy.183
  197.3 7.2 convert_element_type.195
  209.0 325.5 %all-reduce.3.cloned.1.call-done = bf16[4,2,512,512]{3,2,0,1:T(8,128)(2,1)} async-done(((bf16[4,2,512,512]{3,2,0,1:T(8,128)(2,1)}), bf16[4,2,512,512]{3,2,0,1:T(8,128)(2,1)}) %all-reduce.3.cloned.1.call-update) | async-done | bytes 4194320 | tf_op jit(solution)/shard_map/psum | solution.py:159
  539.9 5.0 fusion.103
  547.1 4.7 fusion.81
  551.8 4.5 fusion.93
  556.3 4.5 fusion.94
  562.7 16.0 %all_to_all.47 = bf16[32,2,1024]{2,1,0:T(2,128)(2,1)S(1)} all-to-all(bf16[32,2,1024]{2,1,0:T(2,128)(2,1)S(1)} %reshape.197), channel_id=1, replica_groups=mesh['freq'=4,'vis'=32] {'vis'}, dimensions={0} | all-to-all | bytes 262144 | tf_op jit(solution)/shard_map/all_to_all | solution.py:120
  598.8 33.4 %all_to_all.48 = bf16[32,4,2,512,16]{3,4,2,1,0:T(8,128)(2,1)S(1)} all-to-all(bf16[32,4,2,512,16]{3,4,2,1,0:T(8,128)(2,1)S(1)} %stack.62), channel_id=1, replica_groups=mesh['freq'=4,'vis'=32] {'vis'}, dimensions={0} | all-to-all | bytes 8388608 | tf_op jit(solution)/shard_map/all_to_all | solution.py:124
  634.6 6.9 reshape_reshape.7
  641.6 7.5 copy.132
  649.0 7.3 reshape.163
  660.3 42.9 %while.21 = (s32[]{:T(128)}, f32[64,32768]{1,0:T(8,128)}, s32[2,16]{1,0:T(2,128)S(1)}, s32[2,16]{1,0:T(2,128)S(1)}, bf16[16,32768]{1,0:T(8,128)(2,1)S(1)}, /*ind...) while((s32[]{:T(128)}, f32[64,32768]{1,0:T(8,128)}, ...), condition=%wide.region_6.7_spmd, body=%wide.region_4.6_spmd.sunk | while | flops 1164969216 | bytes 89130760 | solution.py:153
  671.0 10.6 scatter_custom_fusion.11
  692.4 10.6 scatter_custom_fusion.11
  708.4 5.9 copy.182
  714.3 7.2 convert_element_type.201
  721.5 4.4 copy.135
  725.9 320.2 %all-reduce.5.cloned.1.call-done = bf16[4,2,512,512]{3,2,0,1:T(8,128)(2,1)} async-done(((bf16[4,2,512,512]{3,2,0,1:T(8,128)(2,1)}), bf16[4,2,512,512]{3,2,0,1:T(8,128)(2,1)}) %all-reduce.5.cloned.1.call-update) | async-done | bytes 4194320 | tf_op jit(solution)/shard_map/psum | solution.py:159
  1051.5 4.7 fusion.101
  1058.5 5.6 fusion.72
  (182 shorter events, 135.4 us)
Async XLA Ops:
  6.5 5.1 copy-start.6
  57.1 5.1 copy-start.4
  57.1 55.4 %all-to-all-start.1 = ((bf16[32,4,2,512,16]{3,4,2,1,0:T(8,128)(2,1)}), bf16[32,4,2,512,16]{3,4,2,1,0:T(8,128)(2,1)}, u32[]{:S(2)}, u32[]{:S(2)}) async-start(bf16[32,4,2,512,16]{3,4,2,1,0:T(8,128)(2,1)} %stack.55), calls=%async_computation.1 | async-start | bytes 8388608 | tf_op jit(solution)/shard_map/all_to_all | solution.py:124
  62.1 3.0 copy-start.7
  62.1 3.0 copy-start.8
  62.1 3.1 copy-start.9
  62.1 472.4 %all-reduce.3.cloned.1.call-start = ((), (), s32[]{:S(2)}) async-start(), calls=%async_computation.4 | async-start | bytes 8388608 | tf_op jit(solution)/shard_map/psum | solution.py:159
  62.2 1.6 copy-start.5
  143.3 2.2 copy-start.1
  164.7 2.2 copy-start.1
  209.0 837.1 %all-reduce.5.cloned.1.call-start = ((), (), s32[]{:S(2)}) async-start(), calls=%async_computation.5 | async-start | bytes 8388608 | tf_op jit(solution)/shard_map/psum | solution.py:159
  534.5 10.4 copy-start.2
  660.3 2.2 copy-start
  681.6 2.2 copy-start
  1046.1 10.2 copy-start.3
Sparse Core Ops, SparseCore 0:
  209.1 325.3 all-reduce.2
  726.1 319.9 all-reduce.4
